TPU v7x, 256 devices: a whole 4x4x8 slice. The times are simulated.
256 devices in a mesh: bank: 64 (over x_hi, z, y), tp: 4 (over x_lo, core).
Axes of the slice: x: 4 (x_hi: 2, x_lo: 2; x = x_hi * 2 + x_lo), y: 4, z: 8, core: 2. Of those that a mesh axis runs over, the one named last changes fastest.
Arguments:
- hidden: bfloat16 [128, 512, 14336], P('bank', None, 'tp'), may hold values from -6 to 6
- out_grad: bfloat16 [128, 512, 4096], P('bank', None, 'tp'), may hold values from -6 to 6
- proj_in: bfloat16 [64, 14336], P(None, 'tp'), may hold values from -0.046875 to 0.046875
- proj_out: bfloat16 [64, 4096], P(None, 'tp'), may hold values from -0.09375 to 0.09375
- lengths: int32 [128], P('bank'), may hold values from 1 to 512, 49152 in all
- pair_perm: int32 [128], replicated, may hold values from 0 to 127, each once
- bank_slab: bfloat16 [65536, 4096], P('bank', 'tp'), may hold values from -6 to 6
Outputs:
- scores: float32 [64, 65536], P('tp', 'bank')
Inputs may be any that keep to these rules, and one draw needn't show every extreme that they name: pair_perm holds every variant index exactly once. `lengths`: some prompt fills all 512 slots.
All inputs are finite; a program needn't handle non-finite values. No bound on the sum of `lengths` on one device may be relied on, other than what follows from the above.
Results may differ from a plain program's by a relative error of at most 0.0029.
Values sent between devices are 32-bit elements; how exact they have to be, the bound alone decides.
A program may use at most 64 MiB of HBM per device.

v0:
```python
import jax
import jax.numpy as jnp
from jax import lax
from jax.sharding import PartitionSpec as P

epsilon = 1e-06


def per_device(hidden, out_grad, proj_in, proj_out, lengths, pair_perm, bank_slab):
    ex_dev, seq_len, ff_dev = hidden.shape
    factor_rank = proj_in.shape[0]
    tp_count = lax.axis_size("tp")
    share_rows = factor_rank // tp_count
    tok_rows = hidden.reshape(ex_dev * seq_len, ff_dev)
    grad_rows = out_grad.reshape(ex_dev * seq_len, out_grad.shape[2])
    in_part = jnp.einsum("rf,tf->rt", proj_in, tok_rows, preferred_element_type=jnp.float32)
    out_part = jnp.einsum("rd,td->rt", proj_out, grad_rows, preferred_element_type=jnp.float32)
    in_all, out_all = lax.psum((in_part, out_part), "tp")
    in_mine = lax.dynamic_slice_in_dim(in_all, lax.axis_index("tp") * share_rows, share_rows, 0)
    positions = jnp.arange(seq_len, dtype=jnp.int32)
    live_mask = (positions[None, :] < lengths[:, None]).astype(jnp.float32)
    in_three = in_mine.reshape(share_rows, ex_dev, seq_len) * live_mask[None, :, :]
    out_three = out_all.reshape(factor_rank, ex_dev, seq_len)
    grads = jnp.einsum("ies,jes->eij", in_three, out_three, precision=lax.Precision.HIGHEST)
    grads = grads.reshape(ex_dev, share_rows * factor_rank)
    benign = pair_perm[0::2]
    harmful = pair_perm[1::2]
    all_grads = lax.all_gather(grads, "bank", axis=0, tiled=True)
    example_ids = jnp.arange(all_grads.shape[0], dtype=jnp.int32)
    pair_signs = (example_ids[None, :] == harmful[:, None]).astype(jnp.float32) - (
        example_ids[None, :] == benign[:, None]
    ).astype(jnp.float32)
    queries = jnp.dot(pair_signs, all_grads, precision=lax.Precision.HIGHEST)
    query_part = jnp.sum(queries * queries, axis=1)
    slab_wide = bank_slab.astype(jnp.float32)
    bank_part = jnp.sum(slab_wide * slab_wide, axis=1)
    query_sq, bank_sq = lax.psum((query_part, bank_part), "tp")
    query_low = queries.astype(jnp.bfloat16)
    pair_count = queries.shape[0]
    pairs_mine = pair_count // tp_count
    dots = lax.psum_scatter(
        lax.dot_general(
            query_low, bank_slab, (((1,), (1,)), ((), ())), preferred_element_type=jnp.float32
        ),
        "tp",
        scatter_dimension=0,
        tiled=True,
    )
    query_mine = lax.dynamic_slice_in_dim(
        query_sq, lax.axis_index("tp") * pairs_mine, pairs_mine, 0
    )
    return (
        dots
        * factor_rank
        * lax.rsqrt(query_mine + epsilon)[:, None]
        * lax.rsqrt(bank_sq + epsilon)[None, :]
    )


def solution(mesh):
    return jax.shard_map(
        per_device,
        mesh=mesh,
        in_specs=(
            P("bank", None, "tp"),
            P("bank", None, "tp"),
            P(None, "tp"),
            P(None, "tp"),
            P("bank"),
            P(),
            P("bank", "tp"),
        ),
        out_specs=P("tp", "bank"),
        check_vma=False,
    )
```

profile of v0, /device:TPU:1, one launch (start us, length us, event | category | flops | bytes accessed | tf_op | source)
XLA Modules:
  0.0 274.3 jit_solution(10950495381931768916)
XLA Ops:
  6.5 0.0 copy-start
  6.5 0.0 copy-start.1
  6.5 0.0 all-reduce.4.cloned.1.call-start
  6.5 1.6 copy-done
  8.1 1.7 fusion.11
  9.8 0.7 copy.17
  10.5 0.0 copy-done.1
  10.5 0.0 copy-start.3
  10.5 0.0 copy-start.2
  10.5 6.1 %fusion.10 = f32[64,1024]{1,0:T(8,128)} fusion(bf16[64,3584]{1,0:T(8,128)(2,1)S(1)} %copy-done.1, bf16[1024,3584]{1,0:T(8,128)(2,1)} %bitcast.18), kind=kOutput, calls=%fused_computation.21 | convolution fusion | flops 469762048 | bytes 8060928 | tf_op jit(solution)/shard_map/rf,tf->rt/dot_general | solution.py:16
  16.6 0.0 all-reduce.4.cloned.1.call-update
  16.7 0.0 reduce-scatter.2.cloned.1.call-start
  16.7 0.0 copy-done.3
  16.7 0.2 slice.7
  16.9 0.2 slice.6
  17.1 0.0 copy-done.2
  17.1 0.1 compare_convert_fusion
  17.1 46.7 %all-reduce.4.cloned.1.call-done = (f32[64,2,512]{2,0,1:T(8,128)}, f32[64,1024]{1,0:T(8,128)}) async-done(((f32[64,2,512]{2,0,1:T(8,128)}, f32[64,1024]{1,0:T(8,128)}), (f32[64,2,512]{2,0,1:T(8,128)}, f32[64,1024]{1,0:T(8,128)})) %all-reduce.4.cloned.1.call-update) | async-done | bytes 524304 | tf_op jit(solution)/shard_map/psum | solution.py:18
  63.9 0.8 constant_dynamic-slice_fusion
  64.7 0.1 reshape.39
  64.8 1.3 fusion.2
  66.1 0.1 reshape.43
  66.2 156.8 %all-gather = f32[64,2,1024]{2,1,0:T(2,128)S(1)} all-gather(f32[1,2,1024]{2,1,0:T(2,128)S(1)} %reshape.43), channel_id=1, replica_groups=mesh['bank'=64,'tp'=4] {'bank'}, dimensions={0}, use_global_device_ids=true | all-gather | bytes 532480 | tf_op jit(solution)/shard_map/all_gather | solution.py:28
  223.0 0.4 reshape.44
  223.3 0.5 multiply_reduce_fusion.1
  223.9 3.0 %fusion = f32[64,1024]{1,0:T(8,128)} fusion(bf16[1024,1024]{1,0:T(8,128)(2,1)} %param.13, bf16[64,1024]{1,0:T(8,128)(2,1)S(1)} %get-tuple-element.10), kind=kOutput, calls=%fused_computation.3 | convolution fusion | flops 134217728 | bytes 2490368 | tf_op jit(solution)/shard_map/dot_general | solution.py:42
  226.9 0.0 reduce-scatter.2.cloned.1.call-update
  226.9 2.1 multiply_reduce_fusion
  229.0 32.7 %all-reduce = (f32[1024]{0:T(1024)S(1)}, f32[64]{0:T(128)S(1)}) all-reduce(f32[1024]{0:T(1024)S(1)} %multiply_reduce_fusion, f32[64]{0:T(128)S(1)} %get-tuple-element.9), channel_id=1, replica_groups=mesh['bank'=64,'tp'=4] {'tp'}, use_global_device_ids=true, to_apply=%region_6.0 | all-reduce | flops 1088 | bytes 8704 | tf_op jit(solution)/shard_map/psum | solution.py:37
  261.7 0.1 rsqrt_multiply_fusion
  261.8 4.1 %reduce-scatter.2.cloned.1.call-done = f32[16,1024]{1,0:T(8,128)} async-done(((f32[64,1024]{1,0:T(8,128)}), f32[16,1024]{1,0:T(8,128)}) %reduce-scatter.2.cloned.1.call-update) | async-done | bytes 65552 | tf_op jit(solution)/shard_map/reduce_scatter | solution.py:41
  265.9 1.5 multiply_multiply_fusion
  (3 shorter events, 0.0 us)
Async XLA Ops:
  6.5 1.6 copy-start
  6.5 4.0 %copy-start.1 = (bf16[64,3584]{1,0:T(8,128)(2,1)S(1)}, bf16[64,3584]{1,0:T(8,128)(2,1)}, u32[]{:S(2)}) copy-start(bf16[64,3584]{1,0:T(8,128)(2,1)} %param.9) | copy-start | bytes 1376260
  6.5 57.3 %all-reduce.4.cloned.1.call-start = ((), (), s32[]{:S(2)}) async-start(), calls=%async_computation.2 | async-start | bytes 1048576 | tf_op jit(solution)/shard_map/psum | solution.py:18
  10.5 6.2 %copy-start.3 = (s32[128]{0:T(128)S(1)}, s32[128]{0:T(128)}, u32[]{:S(2)}) copy-start(s32[128]{0:T(128)} %param.12) | copy-start | bytes 1540
  10.5 6.5 %copy-start.2 = (s32[2]{0:T(128)S(1)}, s32[2]{0:T(128)}, u32[]{:S(2)}) copy-start(s32[2]{0:T(128)} %param.11) | copy-start | bytes 28
  16.7 249.2 %reduce-scatter.2.cloned.1.call-start = ((), (), s32[]{:S(2)}) async-start(), calls=%async_computation.1 | async-start | bytes 327680 | tf_op jit(solution)/shard_map/reduce_scatter | solution.py:41
Sparse Core Ops, SparseCore 0:
  16.8 47.0 all-reduce.3
  227.1 38.8 reduce-scatter.1
where the time goes:
time: 275 us; the launch traced here: 274 us
  blocking collectives  190 us (69%)
  waiting for transfers between devices  50.9 us (19%)
  between operations  13.5 us (5%)
  matrix products  12.6 us (5%)
  local copies, waits for them, and re-layouts  3.99 us (1%)
  other arithmetic  3.78 us (1%)
    all_gather x1, blocking collectives, per_device(): all_grads = lax.all_gather(grads, 'bank', axis=0, tiled=True)  157 us
    psum x1, waiting for transfers between devices, per_device(): in_all, out_all = lax.psum((in_part, out_part), 'tp')  46.7 us
    psum x1, blocking collectives, per_device(): query_sq, bank_sq = lax.psum((query_part, bank_part), 'tp')  32.7 us
    dot_general x1, matrix products, per_device(): jnp.einsum('rf,tf->rt', proj_in, tok_rows, preferred_element_type=jnp.flo...  6.13 us
  transfers between devices with their start and end apart: 2, of which 2 were waited for; matrix products, arithmetic and copies ran while one was open for 1% of the time, Pallas kernels for 0%

commit v1 on v0

--- a/solution.py
+++ b/solution.py
@@ -25,7 +25,9 @@
     grads = grads.reshape(ex_dev, share_rows * factor_rank)
     benign = pair_perm[0::2]
     harmful = pair_perm[1::2]
-    all_grads = lax.all_gather(grads, "bank", axis=0, tiled=True)
+    all_grads = jnp.concatenate(
+        lax.all_to_all(jnp.stack([grads] * lax.axis_size("bank")), "bank", 0, 0), axis=0
+    )
     example_ids = jnp.arange(all_grads.shape[0], dtype=jnp.int32)
     pair_signs = (example_ids[None, :] == harmful[:, None]).astype(jnp.float32) - (
         example_ids[None, :] == benign[:, None]

time: 275 us -> 127 us (0.46)
  blocking collectives: 190 us -> 7.37 us
  waiting for transfers between devices: 50.9 us -> 71.6 us
  starting transfers between devices: 0.04 us -> 12.4 us
    all_gather x1 -> x0, blocking collectives: 157 us -> none  [per_device(): all_grads = lax.all_gather(grads, 'bank', axis=0, tiled=True)]
    psum x1, blocking collectives: 32.7 us -> 7.37 us  [per_device(): query_sq, bank_sq = lax.psum((query_part, bank_part), 'tp')]
    all_to_all x0 -> x1, waiting for transfers between devices: none -> 17.5 us  [per_device(): lax.all_to_all(jnp.stack([grads] * lax.axis_size('bank')), 'bank', 0, 0)]
    all_to_all x0 -> x1, starting transfers between devices: none -> 12.3 us  [per_device(): lax.all_to_all(jnp.stack([grads] * lax.axis_size('bank')), 'bank', 0, 0)]
    reduce_scatter x1, waiting for transfers between devices: 4.13 us -> 6.93 us  [per_device(): lax.psum_scatter(lax.dot_general(query_low, bank_slab, (((1,), (1,)), (()...]
  transfers between devices with their start and end apart: 2 -> 3, of which waited for: 2 -> 3; matrix products, arithmetic and copies ran while one was open for 1% -> 2% of each run, Pallas kernels for 0% -> 0%
where the time goes in v1:
time: 127 us; the launch traced here: 126 us
  waiting for transfers between devices  71.6 us (56%)
  between operations  13.5 us (11%)
  matrix products  12.6 us (10%)
  starting transfers between devices  12.4 us (10%)
  blocking collectives  7.37 us (6%)
  local copies, waits for them, and re-layouts  4.9 us (4%)
  other arithmetic  3.78 us (3%)
    psum x1, waiting for transfers between devices, per_device(): in_all, out_all = lax.psum((in_part, out_part), 'tp')  47.2 us
    all_to_all x1, waiting for transfers between devices, per_device(): lax.all_to_all(jnp.stack([grads] * lax.axis_size('bank')), 'bank', 0, 0)  17.5 us
    all_to_all x1, starting transfers between devices, per_device(): lax.all_to_all(jnp.stack([grads] * lax.axis_size('bank')), 'bank', 0, 0)  12.3 us
    psum x1, blocking collectives, per_device(): query_sq, bank_sq = lax.psum((query_part, bank_part), 'tp')  7.37 us
    reduce_scatter x1, waiting for transfers between devices, per_device(): lax.psum_scatter(lax.dot_general(query_low, bank_slab, (((1,), (1,)), (()...  6.93 us
    dot_general x1, matrix products, per_device(): jnp.einsum('rf,tf->rt', proj_in, tok_rows, preferred_element_type=jnp.flo...  6.12 us
    dot_general x1, matrix products, per_device(): lax.dot_general(query_low, bank_slab, (((1,), (1,)), ((), ())), preferred...  3.05 us
  transfers between devices with their start and end apart: 3, of which 3 were waited for; matrix products, arithmetic and copies ran while one was open for 2% of the time, Pallas kernels for 0%

profile of v1, /device:TPU:1, one launch (start us, length us, event | category | flops | bytes accessed | tf_op | source)
XLA Modules:
  0.0 126.1 jit_solution(10100173716899101007)
XLA Ops:
  6.5 0.0 copy-start
  6.5 0.0 copy-start.1
  6.5 0.0 all-reduce.4.cloned.1.call-start
  6.5 1.6 %copy-done = bf16[2,512,1024]{2,1,0:T(8,128)(2,1)S(1)} copy-done((bf16[2,512,1024]{2,1,0:T(8,128)(2,1)S(1)}, bf16[2,512,1024]{2,1,0:T(8,128)(2,1)}, u32[]{:S(2)}) %copy-start) | copy-done | bytes 2097176
  8.1 1.7 %fusion.11 = f32[64,1024]{1,0:T(8,128)S(1)} fusion(bf16[64,1024]{1,0:T(8,128)(2,1)} %param.10, bf16[1024,1024]{1,0:T(8,128)(2,1)S(1)} %bitcast.17), kind=kOutput, calls=%fused_computation.22 | convolution fusion | flops 134217728 | bytes 2490368 | tf_op jit(solution)/shard_map/rd,td->rt/dot_general | solution.py:17
  9.8 0.7 copy.15
  10.5 0.0 copy-done.1
  10.5 0.0 copy-start.2
  10.5 6.1 %fusion.10 = f32[64,1024]{1,0:T(8,128)} fusion(bf16[64,3584]{1,0:T(8,128)(2,1)S(1)} %copy-done.1, bf16[1024,3584]{1,0:T(8,128)(2,1)} %bitcast.18), kind=kOutput, calls=%fused_computation.21 | convolution fusion | flops 469762048 | bytes 8060928 | tf_op jit(solution)/shard_map/rf,tf->rt/dot_general | solution.py:16
  16.6 0.0 copy-start.3
  16.6 0.0 all-reduce.4.cloned.1.call-update
  16.6 0.0 copy-done.2
  16.7 0.1 compare_convert_fusion
  16.7 47.2 %all-reduce.4.cloned.1.call-done = (f32[64,2,512]{2,0,1:T(8,128)}, f32[64,1024]{1,0:T(8,128)}) async-done(((f32[64,2,512]{2,0,1:T(8,128)}, f32[64,1024]{1,0:T(8,128)}), (f32[64,2,512]{2,0,1:T(8,128)}, f32[64,1024]{1,0:T(8,128)})) %all-reduce.4.cloned.1.call-update) | async-done | bytes 524304 | tf_op jit(solution)/shard_map/psum | solution.py:18
  63.9 0.8 constant_dynamic-slice_fusion
  64.8 0.1 reshape.41
  64.8 1.3 %fusion.2 = f32[2,16,64]{2,1,0:T(8,128)S(1)} fusion(f32[64,2,512]{2,0,1:T(8,128)} %get-tuple-element.7, f32[16,2,512]{2,1,0:T(2,128)S(1)} %bitcast.22), kind=kOutput, calls=%fused_computation.5 | convolution fusion | flops 12582912 | bytes 335872 | tf_op jit(solution)/shard_map/ies,jes->eij/dot_general | solution.py:24
  66.1 0.1 stack_reshape.2
  66.2 0.9 stack.3
  67.1 12.3 %all-to-all-start = ((f32[64,2,1024]{2,1,0:T(2,128)}), f32[64,2,1024]{2,1,0:T(2,128)S(1)}, u32[]{:S(2)}, u32[]{:S(2)}) async-start(f32[64,2,1024]{2,1,0:T(2,128)} %stack.3), calls=%async_computation | async-start | bytes 1048576 | tf_op jit(solution)/shard_map/all_to_all | solution.py:29
  79.4 0.0 reduce-scatter.2.cloned.1.call-start
  79.5 0.0 copy-done.3
  79.5 0.2 slice.6
  79.7 0.2 slice.7
  79.8 17.5 %all-to-all-done = f32[64,2,1024]{2,1,0:T(2,128)S(1)} async-done(((f32[64,2,1024]{2,1,0:T(2,128)}), f32[64,2,1024]{2,1,0:T(2,128)S(1)}, u32[]{:S(2)}, u32[]{:S(2)}) %all-to-all-start) | async-done | bytes 524320 | tf_op jit(solution)/shard_map/all_to_all | solution.py:29
  97.3 0.4 reshape.44
  97.7 0.5 multiply_reduce_fusion.1
  98.2 3.0 %fusion = f32[64,1024]{1,0:T(8,128)} fusion(bf16[1024,1024]{1,0:T(8,128)(2,1)} %param.13, bf16[64,1024]{1,0:T(8,128)(2,1)S(1)} %get-tuple-element.10), kind=kOutput, calls=%fused_computation.3 | convolution fusion | flops 134217728 | bytes 2490368 | tf_op jit(solution)/shard_map/dot_general | solution.py:44
  101.2 0.0 reduce-scatter.2.cloned.1.call-update
  101.3 2.1 %multiply_reduce_fusion = f32[1024]{0:T(1024)S(1)} fusion(bf16[1024,1024]{1,0:T(8,128)(2,1)} %param.13), kind=kLoop, calls=%fused_computation | loop fusion | flops 3144704 | bytes 2101248 | tf_op jit(solution)/shard_map/reduce_sum | solution.py:38
  103.3 7.4 %all-reduce = (f32[1024]{0:T(1024)S(1)}, f32[64]{0:T(128)S(1)}) all-reduce(f32[1024]{0:T(1024)S(1)} %multiply_reduce_fusion, f32[64]{0:T(128)S(1)} %get-tuple-element.9), channel_id=1, replica_groups=mesh['bank'=64,'tp'=4] {'tp'}, use_global_device_ids=true, to_apply=%region_6.0 | all-reduce | flops 1088 | bytes 8704 | tf_op jit(solution)/shard_map/psum | solution.py:39
  110.7 0.1 rsqrt_multiply_fusion
  110.8 6.9 %reduce-scatter.2.cloned.1.call-done = f32[16,1024]{1,0:T(8,128)} async-done(((f32[64,1024]{1,0:T(8,128)}), f32[16,1024]{1,0:T(8,128)}) %reduce-scatter.2.cloned.1.call-update) | async-done | bytes 65552 | tf_op jit(solution)/shard_map/reduce_scatter | solution.py:43
  117.7 1.5 %multiply_multiply_fusion = f32[16,1024]{1,0:T(8,128)} fusion(f32[16,1024]{1,0:T(8,128)} %reduce-scatter.2.cloned.1.call-done, f32[1024]{0:T(1024)S(1)} %add_rsqrt_fusion, f32[16]{0:T(128)S(1)} %rsqrt_multiply_fusion), kind=kLoop, calls=%fused_computation.7 | loop fusion | flops 32768 | bytes 135232 | tf_op jit(solution)/shard_map/mul | solution.py:55
  (3 shorter events, 0.0 us)
Async XLA Ops:
  6.5 1.6 %copy-start = (bf16[2,512,1024]{2,1,0:T(8,128)(2,1)S(1)}, bf16[2,512,1024]{2,1,0:T(8,128)(2,1)}, u32[]{:S(2)}) copy-start(bf16[2,512,1024]{2,1,0:T(8,128)(2,1)} %param.8) | copy-start | bytes 6291460
  6.5 4.0 %copy-start.1 = (bf16[64,3584]{1,0:T(8,128)(2,1)S(1)}, bf16[64,3584]{1,0:T(8,128)(2,1)}, u32[]{:S(2)}) copy-start(bf16[64,3584]{1,0:T(8,128)(2,1)} %param.9) | copy-start | bytes 1376260
  6.5 57.4 %all-reduce.4.cloned.1.call-start = ((), (), s32[]{:S(2)}) async-start(), calls=%async_computation.3 | async-start | bytes 1048576 | tf_op jit(solution)/shard_map/psum | solution.py:18
  10.5 6.2 %copy-start.2 = (s32[2]{0:T(128)S(1)}, s32[2]{0:T(128)}, u32[]{:S(2)}) copy-start(s32[2]{0:T(128)} %param.11) | copy-start | bytes 28
  16.6 62.9 %copy-start.3 = (s32[128]{0:T(128)S(1)}, s32[128]{0:T(128)}, u32[]{:S(2)}) copy-start(s32[128]{0:T(128)} %param.12) | copy-start | bytes 1540
  67.1 30.2 %all-to-all-start = ((f32[64,2,1024]{2,1,0:T(2,128)}), f32[64,2,1024]{2,1,0:T(2,128)S(1)}, u32[]{:S(2)}, u32[]{:S(2)}) async-start(f32[64,2,1024]{2,1,0:T(2,128)} %stack.3), calls=%async_computation | async-start | bytes 1048576 | tf_op jit(solution)/shard_map/all_to_all | solution.py:29
  79.4 38.3 %reduce-scatter.2.cloned.1.call-start = ((), (), s32[]{:S(2)}) async-start(), calls=%async_computation.2 | async-start | bytes 327680 | tf_op jit(solution)/shard_map/reduce_scatter | solution.py:43
Sparse Core Ops, SparseCore 0:
  16.8 47.0 all-reduce.3
  101.4 16.3 reduce-scatter.1
